TPU v7x, 128 devices: a whole 4x4x4 slice. The times are simulated.
128 devices in a mesh: row: 16 (over y, z_hi, core), col: 8 (over x, z_lo).
Axes of the slice: x: 4, y: 4, z: 4 (z_hi: 2, z_lo: 2; z = z_hi * 2 + z_lo), core: 2. Of those that a mesh axis runs over, the one named last changes fastest.
Arguments:
- aligned_family_embedding: bfloat16 [512, 768, 256], P('row', 'col'), may hold values from -24 to 24
- aligned_slot_available: int32 [512, 768], P('row', 'col'), may hold values from 0 to 1, as said below
- chain_site_available: int32 [768], replicated, may hold values 0 or 1
- duo_embedding: float32 [768, 768, 128], P('row', 'col'), may hold values from -1.2 to 1.2
- averaging_layernorm_stretch: float32 [256], replicated, may hold values from 0.1 to 1.9
- lineup_layernorm_stretch: float32 [256], replicated, may hold values from 0.1 to 1.9
- duo_layernorm_stretch: float32 [128], replicated, may hold values from 0.1 to 1.9
- lefthand_linear_kernel: bfloat16 [256, 32], replicated, may hold values from -0.375 to 0.375
- righthand_linear_kernel: bfloat16 [256, 32], replicated, may hold values from -0.375 to 0.375
- kronecker_linear_kernel: bfloat16 [1024, 128], replicated, may hold values from -0.1875 to 0.1875
- duo_logit_kernel: bfloat16 [128, 8], replicated, may hold values from -0.75 to 0.75
- asker_lookup_sigmoid_kernel: bfloat16 [256, 1024], replicated, may hold values from -8 to 8
- closing_linear_kernel: bfloat16 [256, 256], replicated, may hold values from -0.375 to 0.375
Outputs:
- refreshed_family_embedding: bfloat16 [512, 768, 256], P('row', 'col')
- duo_after_averaging: float32 [768, 768, 128], P('row', 'col')
Inputs may be any that keep to these rules, and one draw needn't show every extreme that they name: `aligned_slot_available`: 0 or 1; sequence 0 is present at every residue.
All inputs are finite; a program needn't handle non-finite values.
Results may differ from a plain program's by a relative error of at most 0.0052.
Values may be sent and summed in bfloat16 or wider, within the bound.
A program may use at most 192 MiB of HBM per device.

v0:
```python
import jax
import jax.numpy as jnp
from jax import lax
from jax.sharding import PartitionSpec as P

EPSILON = 1e-05
CONTRACT_FIRST = (((0,), (0,)), ((), ()))


def laid_out(pieces, dim):
    lengths = list(pieces.shape[1:])
    lengths[dim] *= pieces.shape[0]
    return jnp.moveaxis(pieces, 0, dim).reshape(lengths)


def one_gather(arrays, axis, dims):
    line = jnp.concatenate([a.reshape(-1) for a in arrays])
    lines, at, outs = (lax.all_gather(line, axis), 0, [])
    for a, dim in zip(arrays, dims):
        pieces = lines[:, at : at + a.size].reshape(-1, *a.shape)
        outs.append(laid_out(pieces, dim))
        at += a.size
    return tuple(outs)


def in_one_piece(arrays, axis, dim, along):
    ends, at = ([], 0)
    for a in arrays[:-1]:
        at += a.shape[along]
        ends.append(at)
    both = jnp.concatenate(arrays, axis=along)
    return tuple(jnp.split(lax.all_gather(both, axis, axis=dim, tiled=True), ends, axis=along))


def sent_to_all(x, axis):
    copies = jnp.broadcast_to(x, (lax.axis_size(axis), *x.shape))
    return lax.all_to_all(copies, axis, split_axis=0, concat_axis=0, tiled=True)


def gather_directly(x, axis, dim):
    return laid_out(sent_to_all(x, axis), dim)


def sent_together(arrays, axis, split_dim, concat_dim, along):
    columns = [a.reshape(*a.shape[:along], -1) for a in arrays]
    both = jnp.concatenate(columns, axis=along)
    whole, at, outs = (
        lax.all_to_all(both, axis, split_axis=split_dim, concat_axis=concat_dim, tiled=True),
        0,
        [],
    )
    for a, column in zip(arrays, columns):
        section = whole[..., at : at + column.shape[along]]
        outs.append(section.reshape(*section.shape[:along], *a.shape[along:]))
        at += column.shape[along]
    return tuple(outs)


def standardize_features(values):
    average = jnp.mean(values, axis=-1, keepdims=True)
    centred = values - average
    variance = jnp.mean(centred * centred, axis=-1, keepdims=True)
    return centred * lax.rsqrt(variance + EPSILON)


def project_rows(inputs, weight, availability_real):
    projected = jnp.einsum("src,ca->sra", inputs, weight, preferred_element_type=jnp.float32)
    return (projected * availability_real[:, :, None]).astype(jnp.bfloat16)


def attend(queries, gate_pre, keys_all, values_all, key_mask, bias_rows, head_count):
    homolog_number, query_count, inner_width = queries.shape
    key_count = keys_all.shape[1]
    head_dim = inner_width // head_count
    block_rows = 1
    while (
        block_rows < homolog_number
        and block_rows * query_count < 512
        and (homolog_number % (2 * block_rows) == 0)
    ):
        block_rows = 2 * block_rows
    groups = homolog_number // block_rows
    score_scale = head_dim ** (-0.5)
    bias_float = bias_rows.astype(jnp.float32)

    def one_block(group_members):
        block_query, block_gate, block_key, block_value, block_mask = group_members
        query_heads = block_query.reshape(block_rows, query_count, head_count, head_dim)
        key_heads = block_key.reshape(block_rows, key_count, head_count, head_dim)
        value_heads = block_value.reshape(block_rows, key_count, head_count, head_dim)
        scores = jnp.einsum(
            "bqhd,bkhd->bhqk", query_heads, key_heads, preferred_element_type=jnp.float32
        )
        scores = (
            scores * score_scale
            + bias_float[None]
            + 1000000000.0 * (block_mask.astype(jnp.float32)[:, None, None, :] - 1.0)
        )
        highest = jnp.max(scores, axis=-1, keepdims=True)
        exponent = jnp.exp(scores - highest)
        weights = (exponent / jnp.sum(exponent, axis=-1, keepdims=True)).astype(jnp.bfloat16)
        mixed_rows = jnp.einsum(
            "bhqk,bkhd->bqhd", weights, value_heads, preferred_element_type=jnp.float32
        )
        mixed_rows = mixed_rows.reshape(block_rows, query_count, inner_width)
        return (mixed_rows * jax.nn.sigmoid(block_gate.astype(jnp.float32))).astype(jnp.bfloat16)

    def grouped(array):
        return array.reshape((groups, block_rows) + array.shape[1:])

    gated_row_output = lax.map(
        one_block,
        (
            grouped(queries),
            grouped(gate_pre),
            grouped(keys_all),
            grouped(values_all),
            grouped(key_mask),
        ),
    )
    return gated_row_output.reshape(homolog_number, query_count, inner_width)


def shards(
    aligned_family_embedding,
    aligned_slot_available,
    chain_site_available,
    duo_embedding,
    averaging_layernorm_stretch,
    lineup_layernorm_stretch,
    duo_layernorm_stretch,
    lefthand_linear_kernel,
    righthand_linear_kernel,
    kronecker_linear_kernel,
    duo_logit_kernel,
    asker_lookup_sigmoid_kernel,
    closing_linear_kernel,
):
    homolog_number, amino_position_number, discarded_carry = aligned_family_embedding.shape
    res_rows = duo_embedding.shape[0]
    opm_width = lefthand_linear_kernel.shape[1]
    head_count = duo_logit_kernel.shape[1]
    inner_width = closing_linear_kernel.shape[0]
    row_index = lax.axis_index("row")
    col_index = lax.axis_index("col")
    standardized_features = standardize_features(aligned_family_embedding.astype(jnp.float32))
    availability_real = aligned_slot_available.astype(jnp.float32)
    shrunk_availability = aligned_slot_available.astype(jnp.bfloat16)
    opm_input = (standardized_features * averaging_layernorm_stretch).astype(jnp.bfloat16)
    left_flat = project_rows(opm_input, lefthand_linear_kernel, availability_real).reshape(
        homolog_number, amino_position_number * opm_width
    )
    right_flat = project_rows(opm_input, righthand_linear_kernel, availability_real).reshape(
        homolog_number, amino_position_number * opm_width
    )
    left_wide, mask_wide = one_gather((left_flat, shrunk_availability), "col", (1, 1))
    left_block, left_mask = (
        lax.all_to_all(left_wide, "row", split_axis=1, concat_axis=0, tiled=True),
        lax.all_to_all(mask_wide, "row", split_axis=1, concat_axis=0, tiled=True),
    )
    right_all, mask_all = in_one_piece((right_flat, shrunk_availability), "row", 0, 1)
    outer_sum = lax.dot_general(
        left_block, right_all, CONTRACT_FIRST, preferred_element_type=jnp.float32
    )
    counts = lax.dot_general(
        left_mask, mask_all, CONTRACT_FIRST, preferred_element_type=jnp.float32
    )
    outer_narrow = outer_sum.astype(jnp.bfloat16).reshape(
        res_rows, opm_width, amino_position_number, opm_width
    )
    mixing = kronecker_linear_kernel.reshape(opm_width, opm_width, kronecker_linear_kernel.shape[1])
    update = jnp.einsum("iajb,abk->ijk", outer_narrow, mixing, preferred_element_type=jnp.float32)
    residue_float = chain_site_available.astype(jnp.float32)
    residue_rows = lax.dynamic_slice_in_dim(residue_float, row_index * res_rows, res_rows)
    residue_cols = lax.dynamic_slice_in_dim(
        residue_float, col_index * amino_position_number, amino_position_number
    )
    update = (
        update
        / (counts + 0.001)[:, :, None]
        * (residue_rows[:, None] * residue_cols[None, :])[:, :, None]
    )
    duo_after_averaging = duo_embedding + update
    pair_input = (standardize_features(duo_after_averaging) * duo_layernorm_stretch).astype(
        jnp.bfloat16
    )
    bias_tile = jnp.einsum(
        "ijc,ch->hij", pair_input, duo_logit_kernel, preferred_element_type=jnp.float32
    ).astype(jnp.bfloat16)
    bias_cols = gather_directly(bias_tile, "col", 2)
    exponential_probabilities = (standardized_features * lineup_layernorm_stretch).astype(
        jnp.bfloat16
    )
    rows_input, rows_mask = sent_together(
        (exponential_probabilities, shrunk_availability), "col", 0, 1, 2
    )
    bias_whole = lax.all_gather(bias_cols, "row", axis=1, tiled=True)
    projected = jnp.einsum(
        "src,cd->srd", rows_input, asker_lookup_sigmoid_kernel, preferred_element_type=jnp.float32
    ).astype(jnp.bfloat16)
    gated_whole = attend(
        projected[..., :inner_width],
        projected[..., 3 * inner_width :],
        projected[..., inner_width : 2 * inner_width],
        projected[..., 2 * inner_width : 3 * inner_width],
        rows_mask,
        bias_whole,
        head_count,
    )
    gated_local = lax.all_to_all(gated_whole, "col", split_axis=1, concat_axis=0, tiled=True)
    summed_increment = jnp.einsum(
        "sqd,dc->sqc", gated_local, closing_linear_kernel, preferred_element_type=jnp.float32
    )
    refreshed_family_embedding = (
        aligned_family_embedding.astype(jnp.float32) + summed_increment
    ).astype(jnp.bfloat16)
    return (refreshed_family_embedding, duo_after_averaging)


def solution(mesh):
    placed = (
        P("row", "col", None),
        P("row", "col"),
        P(),
        P("row", "col", None),
        P(),
        P(),
        P(),
        P(),
        P(),
        P(),
        P(),
        P(),
        P(),
    )
    return jax.shard_map(
        shards,
        mesh=mesh,
        in_specs=placed,
        out_specs=(P("row", "col", None), P("row", "col", None)),
        check_vma=False,
    )
```

profile of v0, /device:TPU:0, one launch (start us, length us, event | category | flops | bytes accessed | tf_op | source)
XLA Modules:
  0.0 554.7 jit_solution(972236072395999321)
XLA Ops:
  16.7 43.4 %all-gather.9.cloned.1.call-done = bf16[811008]{0:T(1024)(128)(2,1)} async-done(((bf16[101376]{0:T(1024)(128)(2,1)}), bf16[811008]{0:T(1024)(128)(2,1)}) %all-gather.9.cloned.1.call-update) | async-done | bytes 1622032 | tf_op jit(solution)/shard_map/all_gather | solution.py:18
  89.2 25.7 %all-to-all-done.1 = bf16[32,16,1536]{2,0,1:T(8,128)(2,1)} async-done(((bf16[32,16,1536]{2,0,1:T(8,128)(2,1)}), bf16[32,16,1536]{2,0,1:T(8,128)(2,1)}, u32[]{:S(2)}, u32[]{:S(2)}) %all-to-all-start.1) | async-done | bytes 1572896 | tf_op jit(solution)/shard_map/all_to_all | solution.py:158
  114.9 13.3 %all-gather.5.cloned.1.call-done = bf16[512,3168]{1,0:T(8,128)(2,1)} async-done(((bf16[32,3168]{1,0:T(8,128)(2,1)}), bf16[512,3168]{1,0:T(8,128)(2,1)}) %all-gather.5.cloned.1.call-update) | async-done | bytes 3244048 | tf_op jit(solution)/shard_map/all_gather | solution.py:32
  128.2 9.5 %convolution_convert_fusion = bf16[1536,3072]{1,0:T(8,128)(2,1)} fusion(bf16[512,1536]{1,0:T(8,128)(2,1)} %bitcast.18, bf16[512,3168]{1,0:T(8,128)(2,1)} %all-gather.5.cloned.1.call-done), kind=kOutput, calls=%fused_computation.13 | convolution fusion | flops 4836556800 | bytes 14155776 | tf_op jit(solution)/shard_map/dot_general | solution.py:162
  137.7 41.0 %reshape.210 = bf16[48,32,96,32]{3,2,1,0:T(8,128)(2,1)} reshape(bf16[1536,3072]{1,0:T(8,128)(2,1)} %convolution_convert_fusion) | data formatting | bytes 18874368 | tf_op jit(solution)/shard_map/reshape | solution.py:168
  179.8 17.1 %fusion.31 = (f32[48,96]{1,0:T(8,128)S(1)}, f32[48,96,128]{2,1,0:T(8,128)S(1)}) fusion(f32[48,96,128]{2,1,0:T(8,128)} %param.18, f32[48,96]{1,0:T(8,128)S(1)} %broadcast_multiply_fusion.1, f32[48,96]{1,0:T(8,128)S(1)} %convolution_add_fusion, bf16[48,32,96,32]{3,2,1,0:T(8,128)(2,1)} %reshape.210, bf16[32,32,128,1]{2,1,0,3:T(8,128)(2,1)S(1)} %bitcast.115), kind=kOutput, calls=%fused_computation.62 | convolution fusion | flops 1210314240 | bytes 14473216 | tf_op jit(solution)/shard_map/iajb,abk->ijk/dot_general | solution.py:172
  200.8 16.6 %all_to_all.79 = bf16[8,8,48,96]{3,2,1,0:T(8,128)(2,1)S(1)} all-to-all(bf16[8,8,48,96]{3,2,1,0:T(8,128)(2,1)S(1)} %broadcast_in_dim.6), channel_id=1, replica_groups=mesh['row'=16,'col'=8] {'col'}, dimensions={0} | all-to-all | bytes 1179648 | tf_op jit(solution)/shard_map/all_to_all | solution.py:37
  231.5 30.3 %all-to-all-done = bf16[32,96,257]{1,2,0:T(8,128)(2,1)} async-done(((bf16[32,96,257]{1,2,0:T(8,128)(2,1)}), bf16[32,96,257]{1,2,0:T(8,128)(2,1)}, u32[]{:S(2)}, u32[]{:S(2)}) %all-to-all-start) | async-done | bytes 1579040 | tf_op jit(solution)/shard_map/all_to_all | solution.py:48
  273.7 41.4 %all-gather.7.cloned.1.call-done = bf16[8,768,768]{2,0,1:T(8,128)(2,1)} async-done(((bf16[8,48,768]{2,0,1:T(8,128)(2,1)}), bf16[8,768,768]{2,0,1:T(8,128)(2,1)}) %all-gather.7.cloned.1.call-update) | async-done | bytes 9437200 | tf_op jit(solution)/shard_map/all_gather | solution.py:197
  315.1 15.4 %copy.95 = f32[8,768,768]{1,2,0:T(8,128)} copy(bf16[8,768,768]{2,0,1:T(8,128)(2,1)} %all-gather.7.cloned.1.call-done) | data formatting | bytes 28311552 | tf_op jit(solution)/shard_map/while | solution.py:111
  330.5 186.1 %while.12 = (s32[]{:T(128)}, bf16[4,1,768,256]{2,3,1,0:T(8,128)(2,1)}, bf16[4,1,768,256]{3,2,0,1:T(8,128)(2,1)}, bf16[4,1,768,256]{3,2,0,1:T(8,128)(2,1)}, bf16[...) while((s32[]{:T(128)}, ...), condition=%wide.region_7.8_spmd, body=%wide.region_4.7_spmd.sunk | while | flops 642918144 | bytes 85385320 | solution.py:111
  333.2 12.1 %add_add_fusion.2 = f32[8,768,768]{1,2,0:T(8,128)} fusion(f32[8,768,768]{1,2,0:T(8,128)} %get-tuple-element.252, f32[768]{0:T(1024)S(1)} %multiply_reduce_fusion.3, bf16[768,8,32]{0,2,1:T(8,128)(2,1)S(1)} %bitcast.100, bf16[768,8,32]{0,2,1:T(8,128)(2,1)S(1)} %bitcast.101), kind=kOutput, calls=%fused_computation.3.clone.1 | convolution fusion | flops 316145664 | bytes 38538240 | tf_op jit(solution)/shard_map/while/body/eval_jaxpr/bqhd,bkhd->bhqk/dot_general | solution.py:91
  345.3 13.7 %fusion.55 = f32[8,768]{1,0:T(8,128)S(1)} fusion(f32[8,768,768]{1,2,0:T(8,128)} %add_add_fusion.2), kind=kOutput, calls=%fused_computation.60.clone.1 | output fusion | flops 9437951 | bytes 18898944 | tf_op jit(solution)/shard_map/while/body/eval_jaxpr/sub | solution.py:100
  359.2 16.6 %fusion.56 = f32[8,32,768]{2,1,0:T(8,128)S(1)} fusion(bf16[768,8,32]{0,2,1:T(8,128)(2,1)S(1)} %bitcast.103, f32[8,768]{1,0:T(8,128)S(1)} %fusion.55, f32[8,768,768]{1,2,0:T(8,128)} %add_add_fusion.2), kind=kOutput, calls=%fused_computation.4.clone.1 | convolution fusion | flops 316152576 | bytes 20078592 | tf_op jit(solution)/shard_map/while/body/eval_jaxpr/bhqk,bkhd->bqhd/dot_general | solution.py:102
  379.8 12.1 %add_add_fusion.2 = f32[8,768,768]{1,2,0:T(8,128)} fusion(f32[8,768,768]{1,2,0:T(8,128)} %get-tuple-element.252, f32[768]{0:T(1024)S(1)} %multiply_reduce_fusion.3, bf16[768,8,32]{0,2,1:T(8,128)(2,1)S(1)} %bitcast.100, bf16[768,8,32]{0,2,1:T(8,128)(2,1)S(1)} %bitcast.101), kind=kOutput, calls=%fused_computation.3.clone.1 | convolution fusion | flops 316145664 | bytes 38538240 | tf_op jit(solution)/shard_map/while/body/eval_jaxpr/bqhd,bkhd->bhqk/dot_general | solution.py:91
  391.9 13.7 %fusion.55 = f32[8,768]{1,0:T(8,128)S(1)} fusion(f32[8,768,768]{1,2,0:T(8,128)} %add_add_fusion.2), kind=kOutput, calls=%fused_computation.60.clone.1 | output fusion | flops 9437951 | bytes 18898944 | tf_op jit(solution)/shard_map/while/body/eval_jaxpr/sub | solution.py:100
  405.8 16.6 %fusion.56 = f32[8,32,768]{2,1,0:T(8,128)S(1)} fusion(bf16[768,8,32]{0,2,1:T(8,128)(2,1)S(1)} %bitcast.103, f32[8,768]{1,0:T(8,128)S(1)} %fusion.55, f32[8,768,768]{1,2,0:T(8,128)} %add_add_fusion.2), kind=kOutput, calls=%fused_computation.4.clone.1 | convolution fusion | flops 316152576 | bytes 20078592 | tf_op jit(solution)/shard_map/while/body/eval_jaxpr/bhqk,bkhd->bqhd/dot_general | solution.py:102
  426.3 12.1 %add_add_fusion.2 = f32[8,768,768]{1,2,0:T(8,128)} fusion(f32[8,768,768]{1,2,0:T(8,128)} %get-tuple-element.252, f32[768]{0:T(1024)S(1)} %multiply_reduce_fusion.3, bf16[768,8,32]{0,2,1:T(8,128)(2,1)S(1)} %bitcast.100, bf16[768,8,32]{0,2,1:T(8,128)(2,1)S(1)} %bitcast.101), kind=kOutput, calls=%fused_computation.3.clone.1 | convolution fusion | flops 316145664 | bytes 38538240 | tf_op jit(solution)/shard_map/while/body/eval_jaxpr/bqhd,bkhd->bhqk/dot_general | solution.py:91
  438.4 13.7 %fusion.55 = f32[8,768]{1,0:T(8,128)S(1)} fusion(f32[8,768,768]{1,2,0:T(8,128)} %add_add_fusion.2), kind=kOutput, calls=%fused_computation.60.clone.1 | output fusion | flops 9437951 | bytes 18898944 | tf_op jit(solution)/shard_map/while/body/eval_jaxpr/sub | solution.py:100
  452.3 16.6 %fusion.56 = f32[8,32,768]{2,1,0:T(8,128)S(1)} fusion(bf16[768,8,32]{0,2,1:T(8,128)(2,1)S(1)} %bitcast.103, f32[8,768]{1,0:T(8,128)S(1)} %fusion.55, f32[8,768,768]{1,2,0:T(8,128)} %add_add_fusion.2), kind=kOutput, calls=%fused_computation.4.clone.1 | convolution fusion | flops 316152576 | bytes 20078592 | tf_op jit(solution)/shard_map/while/body/eval_jaxpr/bhqk,bkhd->bqhd/dot_general | solution.py:102
  472.8 12.1 %add_add_fusion.2 = f32[8,768,768]{1,2,0:T(8,128)} fusion(f32[8,768,768]{1,2,0:T(8,128)} %get-tuple-element.252, f32[768]{0:T(1024)S(1)} %multiply_reduce_fusion.3, bf16[768,8,32]{0,2,1:T(8,128)(2,1)S(1)} %bitcast.100, bf16[768,8,32]{0,2,1:T(8,128)(2,1)S(1)} %bitcast.101), kind=kOutput, calls=%fused_computation.3.clone.1 | convolution fusion | flops 316145664 | bytes 38538240 | tf_op jit(solution)/shard_map/while/body/eval_jaxpr/bqhd,bkhd->bhqk/dot_general | solution.py:91
  484.9 13.7 %fusion.55 = f32[8,768]{1,0:T(8,128)S(1)} fusion(f32[8,768,768]{1,2,0:T(8,128)} %add_add_fusion.2), kind=kOutput, calls=%fused_computation.60.clone.1 | output fusion | flops 9437951 | bytes 18898944 | tf_op jit(solution)/shard_map/while/body/eval_jaxpr/sub | solution.py:100
  498.8 16.6 %fusion.56 = f32[8,32,768]{2,1,0:T(8,128)S(1)} fusion(bf16[768,8,32]{0,2,1:T(8,128)(2,1)S(1)} %bitcast.103, f32[8,768]{1,0:T(8,128)S(1)} %fusion.55, f32[8,768,768]{1,2,0:T(8,128)} %add_add_fusion.2), kind=kOutput, calls=%fused_computation.4.clone.1 | convolution fusion | flops 316152576 | bytes 20078592 | tf_op jit(solution)/shard_map/while/body/eval_jaxpr/bhqk,bkhd->bqhd/dot_general | solution.py:102
  519.3 25.5 %all_to_all.80 = bf16[4,768,256]{2,0,1:T(4,128)(2,1)S(1)} all-to-all(bf16[4,768,256]{2,0,1:T(4,128)(2,1)S(1)} %bitcast.107), channel_id=1, replica_groups=mesh['row'=16,'col'=8] {'col'}, dimensions={1} | all-to-all | bytes 3145728 | tf_op jit(solution)/shard_map/all_to_all | solution.py:210
  (124 shorter events, 91.4 us)
Async XLA Ops:
  7.2 260.4 %copy-start = (bf16[256,1024]{1,0:T(8,128)(2,1)S(1)}, bf16[256,1024]{1,0:T(8,128)(2,1)}, u32[]{:S(2)}) copy-start(bf16[256,1024]{1,0:T(8,128)(2,1)} %param.26) | copy-start | bytes 1572868
  7.2 2.3 copy-start.2
  7.2 3.3 copy-start.6
  7.2 3.3 copy-start.14
  7.2 3.3 copy-start.12
  7.2 52.8 %all-gather.9.cloned.1.call-start = ((), (), s32[]{:S(2)}) async-start(), calls=%async_computation.7 | async-start | bytes 1824768 | tf_op jit(solution)/shard_map/all_gather | solution.py:18
  10.6 2.9 copy-start.13
  13.4 114.8 %all-gather.5.cloned.1.call-start = ((), (), s32[]{:S(2)}) async-start(), calls=%async_computation.5 | async-start | bytes 3481600 | tf_op jit(solution)/shard_map/all_gather | solution.py:32
  65.3 15.9 %all-to-all-start.2 = ((bf16[16,2,768]{2,1,0:T(2,128)(2,1)}), bf16[16,2,768]{2,1,0:T(2,128)(2,1)S(1)}, u32[]{:S(2)}, u32[]{:S(2)}) async-start(bf16[16,2,768]{2,1,0:T(2,128)(2,1)} %reshape.227), calls=%async_computation.2 | async-start | bytes 98304 | tf_op jit(solution)/shard_map/all_to_all | solution.py:159
  81.1 7.6 %copy-start.7 = (s32[768]{0:T(1024)S(1)}, s32[768]{0:T(1024)}, u32[]{:S(2)}) copy-start(s32[768]{0:T(1024)} %param.17) | copy-start | bytes 9220
  81.1 33.8 %all-to-all-start.1 = ((bf16[32,16,1536]{2,0,1:T(8,128)(2,1)}), bf16[32,16,1536]{2,0,1:T(8,128)(2,1)}, u32[]{:S(2)}, u32[]{:S(2)}) async-start(bf16[32,16,1536]{2,0,1:T(8,128)(2,1)} %copy.83), calls=%async_computation.1 | async-start | bytes 3145728 | tf_op jit(solution)/shard_map/all_to_all | solution.py:158
  88.5 226.6 %all-gather.7.cloned.1.call-start = ((), (), s32[]{:S(2)}) async-start(), calls=%async_computation.6 | async-start | bytes 10027008 | tf_op jit(solution)/shard_map/all_gather | solution.py:197
  137.7 42.1 %copy-start.11 = (bf16[1024,128]{1,0:T(8,128)(2,1)S(1)}, bf16[1024,128]{1,0:T(8,128)(2,1)}, u32[]{:S(2)}) copy-start(bf16[1024,128]{1,0:T(8,128)(2,1)} %param.24) | copy-start | bytes 786436
  196.9 3.7 copy-start.4
  196.9 1.7 copy-start.8
  196.9 1.7 copy-start.10
  217.4 2.4 copy-start.9
  226.9 34.9 %all-to-all-start = ((bf16[32,96,257]{1,2,0:T(8,128)(2,1)}), bf16[32,96,257]{1,2,0:T(8,128)(2,1)}, u32[]{:S(2)}, u32[]{:S(2)}) async-start(bf16[32,96,257]{1,2,0:T(8,128)(2,1)} %copy.80), calls=%async_computation | async-start | bytes 4325376 | tf_op jit(solution)/shard_map/all_to_all | solution.py:48
  545.1 1.4 copy-start.3
  545.1 1.4 copy-start.5
  545.2 3.0 copy-start.1
Sparse Core Ops, SparseCore 0:
  13.6 46.4 all-gather.8
  62.5 65.7 all-gather.4
  219.5 95.5 all-gather.6
where the time goes:
time: 557 us; the launch traced here: 555 us
  waiting for transfers between devices  154 us (28%)
  matrix products  152 us (27%)
  local copies, waits for them, and re-layouts  106 us (19%)
  other arithmetic  68 us (12%)
  blocking collectives  42.1 us (8%)
  starting transfers between devices  18.4 us (3%)
  between operations  14.2 us (3%)
    dot_general x4, matrix products, one_block(): jnp.einsum('bhqk,bkhd->bqhd', weights, value_heads, preferred_element_typ...  66.6 us
    sub x4, other arithmetic, one_block(): exponent = jnp.exp(scores - highest)  54.9 us
    dot_general x4, matrix products, one_block(): jnp.einsum('bqhd,bkhd->bhqk', query_heads, key_heads, preferred_element_t...  48.4 us
    all_gather x1, waiting for transfers between devices, one_gather(): lines, at, outs = (lax.all_gather(line, axis), 0, [])  43.4 us
    all_gather x1, waiting for transfers between devices, shards(): bias_whole = lax.all_gather(bias_cols, 'row', axis=1, tiled=True)  41.4 us
    reshape x1, local copies, waits for them, and re-layouts, shards(): outer_sum.astype(jnp.bfloat16)  41 us
    all_to_all x1, waiting for transfers between devices, sent_together(): lax.all_to_all(both, axis, split_axis=split_dim, concat_axis=concat_dim,...  30.3 us
    all_to_all x1, waiting for transfers between devices, shards(): lax.all_to_all(left_wide, 'row', split_axis=1, concat_axis=0, tiled=True)  25.7 us
  transfers between devices with their start and end apart: 6, of which 5 were waited for; matrix products, arithmetic and copies ran while one was open for 6% of the time, Pallas kernels for 0%

commit v1 on v0

--- a/solution.py
+++ b/solution.py
@@ -1,3 +1,4 @@
+import functools
 import jax
 import jax.numpy as jnp
 from jax import lax
@@ -5,6 +6,15 @@
 
 EPSILON = 1e-05
 CONTRACT_FIRST = (((0,), (0,)), ((), ()))
+
+
+def store_the_ranges(xx, axis_name):
+    return jnp.concatenate(
+        jax.lax.all_to_all(jnp.stack(jax.lax.psum(1, axis_name) * [xx], 0), axis_name, 0, 0), 1
+    )
+
+
+rates_work = functools.partial(store_the_ranges, axis_name="row")
 
 
 def laid_out(pieces, dim):
@@ -194,7 +204,7 @@
     rows_input, rows_mask = sent_together(
         (exponential_probabilities, shrunk_availability), "col", 0, 1, 2
     )
-    bias_whole = lax.all_gather(bias_cols, "row", axis=1, tiled=True)
+    bias_whole = rates_work(bias_cols)
     projected = jnp.einsum(
         "src,cd->srd", rows_input, asker_lookup_sigmoid_kernel, preferred_element_type=jnp.float32
     ).astype(jnp.bfloat16)

time: 557 us -> 675 us (1.21)
  waiting for transfers between devices: 154 us -> 259 us
  blocking collectives: 42.1 us -> 23 us
  other arithmetic: 68 us -> 80.8 us
  starting transfers between devices: 18.4 us -> 26.5 us
  local copies, waits for them, and re-layouts: 106 us -> 114 us
    all_to_all x0 -> x2, waiting for transfers between devices: none -> 148 us  [the longest x1 140 us: store_the_ranges(): jax.lax.all_to_all(jnp.stack(jax.lax.psum(1, axis_name) * [xx], 0), axis_...]
    all_gather x1 -> x0, waiting for transfers between devices: 41.4 us -> none  [shards(): bias_whole = lax.all_gather(bias_cols, 'row', axis=1, tiled=True)]
    all_to_all x1 -> x0, blocking collectives: 16.6 us -> none  [sent_to_all(): return lax.all_to_all(copies, axis, split_axis=0, concat_axis=0, tiled=True)]
    convert_element_type x0 -> x1, other arithmetic: none -> 12.8 us  [attend(): bias_float = bias_rows.astype(jnp.float32)]
    all_to_all x0 -> x2, starting transfers between devices: none -> 9.22 us  [the longest x1 5.01 us: store_the_ranges(): jax.lax.all_to_all(jnp.stack(jax.lax.psum(1, axis_name) * [xx], 0), axis_...]
    another operation x0 -> x2, local copies, waits for them, and re-layouts: none -> 7.49 us  [store_the_ranges(): jnp.stack(jax.lax.psum(1, axis_name) * [xx], 0)]
  transfers between devices with their start and end apart: 6 -> 7, of which waited for: 5 -> 6; matrix products, arithmetic and copies ran while one was open for 6% -> 5% of each run, Pallas kernels for 0% -> 0%
where the time goes in v1:
time: 675 us; the launch traced here: 670 us
  waiting for transfers between devices  259 us (38%)
  matrix products  152 us (23%)
  local copies, waits for them, and re-layouts  114 us (17%)
  other arithmetic  80.8 us (12%)
  starting transfers between devices  26.5 us (4%)
  blocking collectives  23 us (3%)
  between operations  14.5 us (2%)
    all_to_all x1, waiting for transfers between devices, store_the_ranges(): jax.lax.all_to_all(jnp.stack(jax.lax.psum(1, axis_name) * [xx], 0), axis_...  140 us
    dot_general x4, matrix products, one_block(): jnp.einsum('bhqk,bkhd->bqhd', weights, value_heads, preferred_element_typ...  66.6 us
    sub x4, other arithmetic, one_block(): exponent = jnp.exp(scores - highest)  54.9 us
    dot_general x4, matrix products, one_block(): jnp.einsum('bqhd,bkhd->bhqk', query_heads, key_heads, preferred_element_t...  48.6 us
    all_gather x1, waiting for transfers between devices, one_gather(): lines, at, outs = (lax.all_gather(line, axis), 0, [])  43.3 us
    reshape x1, local copies, waits for them, and re-layouts, shards(): outer_sum.astype(jnp.bfloat16)  41 us
    all_to_all x1, waiting for transfers between devices, sent_together(): lax.all_to_all(both, axis, split_axis=split_dim, concat_axis=concat_dim,...  28.7 us
    all_to_all x1, waiting for transfers between devices, shards(): lax.all_to_all(left_wide, 'row', split_axis=1, concat_axis=0, tiled=True)  25.9 us
  transfers between devices with their start and end apart: 7, of which 6 were waited for; matrix products, arithmetic and copies ran while one was open for 5% of the time, Pallas kernels for 0%

profile of v1, /device:TPU:0, one launch (start us, length us, event | category | flops | bytes accessed | tf_op | source)
XLA Modules:
  0.0 670.1 jit_solution(11215026353240403487)
XLA Ops:
  16.7 43.3 %all-gather.6.cloned.1.call-done = bf16[811008]{0:T(1024)(128)(2,1)} async-done(((bf16[101376]{0:T(1024)(128)(2,1)}), bf16[811008]{0:T(1024)(128)(2,1)}) %all-gather.6.cloned.1.call-update) | async-done | bytes 1622032 | tf_op jit(solution)/shard_map/all_gather | solution.py:28
  89.0 25.9 %all-to-all-done.1 = bf16[32,16,1536]{2,0,1:T(8,128)(2,1)} async-done(((bf16[32,16,1536]{2,0,1:T(8,128)(2,1)}), bf16[32,16,1536]{2,0,1:T(8,128)(2,1)}, u32[]{:S(2)}, u32[]{:S(2)}) %all-to-all-start.1) | async-done | bytes 1572896 | tf_op jit(solution)/shard_map/all_to_all | solution.py:168
  114.9 13.3 %all-gather.4.cloned.1.call-done = bf16[512,3168]{1,0:T(8,128)(2,1)} async-done(((bf16[32,3168]{1,0:T(8,128)(2,1)}), bf16[512,3168]{1,0:T(8,128)(2,1)}) %all-gather.4.cloned.1.call-update) | async-done | bytes 3244048 | tf_op jit(solution)/shard_map/all_gather | solution.py:42
  128.2 9.5 %convolution_convert_fusion = bf16[1536,3072]{1,0:T(8,128)(2,1)} fusion(bf16[512,1536]{1,0:T(8,128)(2,1)} %bitcast.18, bf16[512,3168]{1,0:T(8,128)(2,1)} %all-gather.4.cloned.1.call-done), kind=kOutput, calls=%fused_computation.13 | convolution fusion | flops 4836556800 | bytes 14155776 | tf_op jit(solution)/shard_map/dot_general | solution.py:172
  137.7 41.0 %reshape.213 = bf16[48,32,96,32]{3,2,1,0:T(8,128)(2,1)} reshape(bf16[1536,3072]{1,0:T(8,128)(2,1)} %convolution_convert_fusion) | data formatting | bytes 18874368 | tf_op jit(solution)/shard_map/reshape | solution.py:178
  179.8 18.3 %fusion.31 = (f32[48,96]{1,0:T(8,128)S(1)}, f32[48,96,128]{2,1,0:T(8,128)}) fusion(f32[48,96,128]{2,1,0:T(8,128)} %param.18, f32[48,96]{1,0:T(8,128)S(1)} %broadcast_multiply_fusion.1, f32[48,96]{1,0:T(8,128)S(1)} %convolution_add_fusion, bf16[48,32,96,32]{3,2,1,0:T(8,128)(2,1)} %reshape.213, bf16[32,32,128,1]{2,1,0,3:T(8,128)(2,1)S(1)} %bitcast.117), kind=kOutput, calls=%fused_computation.63 | convolution fusion | flops 1210314240 | bytes 14473216 | tf_op jit(solution)/shard_map/iajb,abk->ijk/dot_general | solution.py:182
  228.7 28.7 %all-to-all-done = bf16[32,96,257]{1,2,0:T(8,128)(2,1)S(1)} async-done(((bf16[32,96,257]{1,2,0:T(8,128)(2,1)}), bf16[32,96,257]{1,2,0:T(8,128)(2,1)S(1)}, u32[]{:S(2)}, u32[]{:S(2)}) %all-to-all-start) | async-done | bytes 1579040 | tf_op jit(solution)/shard_map/all_to_all | solution.py:58
  276.6 139.8 %all-to-all-done.4 = bf16[16,8,48,768]{3,2,1,0:T(8,128)(2,1)} async-done(((bf16[16,8,48,768]{3,2,1,0:T(8,128)(2,1)}), bf16[16,8,48,768]{3,2,1,0:T(8,128)(2,1)}, u32[]{:S(2)}, u32[]{:S(2)}) %all-to-all-start.4) | async-done | bytes 9437216 | tf_op jit(solution)/shard_map/all_to_all | solution.py:13
  416.4 12.8 %copy_convert_fusion = f32[16,8,48,768]{3,2,0,1:T(8,128)} fusion(bf16[16,8,48,768]{3,2,1,0:T(8,128)(2,1)} %all-to-all-done.4), kind=kLoop, calls=%fused_computation.14 | loop fusion | flops 4718592 | bytes 28311552 | tf_op jit(solution)/shard_map/convert_element_type | solution.py:94
  429.2 18.7 %copy.98 = f32[8,768,768]{1,2,0:T(8,128)} copy(f32[8,768,768]{2,1,0:T(8,128)} %bitcast.101) | data formatting | bytes 37748736 | tf_op jit(solution)/shard_map/while | solution.py:121
  447.8 186.3 %while.12 = (s32[]{:T(128)}, bf16[4,1,768,256]{2,3,1,0:T(8,128)(2,1)}, bf16[4,1,768,256]{3,2,0,1:T(8,128)(2,1)}, bf16[4,1,768,256]{3,2,0,1:T(8,128)(2,1)}, bf16[...) while((s32[]{:T(128)}, ...), condition=%wide.region_7.8_spmd, body=%wide.region_4.7_spmd.sunk | while | flops 642918144 | bytes 85385320 | solution.py:121
  450.6 12.1 %add_add_fusion.2 = f32[8,768,768]{1,2,0:T(8,128)} fusion(f32[8,768,768]{1,2,0:T(8,128)} %get-tuple-element.252, f32[768]{0:T(1024)S(1)} %multiply_reduce_fusion.3, bf16[768,8,32]{0,2,1:T(8,128)(2,1)S(1)} %bitcast.102, bf16[768,8,32]{0,2,1:T(8,128)(2,1)S(1)} %bitcast.103), kind=kOutput, calls=%fused_computation.3.clone.1 | convolution fusion | flops 316145664 | bytes 38538240 | tf_op jit(solution)/shard_map/while/body/eval_jaxpr/bqhd,bkhd->bhqk/dot_general | solution.py:101
  462.7 13.7 %fusion.55 = f32[8,768]{1,0:T(8,128)S(1)} fusion(f32[8,768,768]{1,2,0:T(8,128)} %add_add_fusion.2), kind=kOutput, calls=%fused_computation.61.clone.1 | output fusion | flops 9437951 | bytes 18898944 | tf_op jit(solution)/shard_map/while/body/eval_jaxpr/sub | solution.py:110
  476.6 16.6 %fusion.56 = f32[8,32,768]{2,1,0:T(8,128)S(1)} fusion(bf16[768,8,32]{0,2,1:T(8,128)(2,1)S(1)} %bitcast.105, f32[8,768]{1,0:T(8,128)S(1)} %fusion.55, f32[8,768,768]{1,2,0:T(8,128)} %add_add_fusion.2), kind=kOutput, calls=%fused_computation.4.clone.1 | convolution fusion | flops 316152576 | bytes 20078592 | tf_op jit(solution)/shard_map/while/body/eval_jaxpr/bhqk,bkhd->bqhd/dot_general | solution.py:112
  497.1 12.1 %add_add_fusion.2 = f32[8,768,768]{1,2,0:T(8,128)} fusion(f32[8,768,768]{1,2,0:T(8,128)} %get-tuple-element.252, f32[768]{0:T(1024)S(1)} %multiply_reduce_fusion.3, bf16[768,8,32]{0,2,1:T(8,128)(2,1)S(1)} %bitcast.102, bf16[768,8,32]{0,2,1:T(8,128)(2,1)S(1)} %bitcast.103), kind=kOutput, calls=%fused_computation.3.clone.1 | convolution fusion | flops 316145664 | bytes 38538240 | tf_op jit(solution)/shard_map/while/body/eval_jaxpr/bqhd,bkhd->bhqk/dot_general | solution.py:101
  509.3 13.7 %fusion.55 = f32[8,768]{1,0:T(8,128)S(1)} fusion(f32[8,768,768]{1,2,0:T(8,128)} %add_add_fusion.2), kind=kOutput, calls=%fused_computation.61.clone.1 | output fusion | flops 9437951 | bytes 18898944 | tf_op jit(solution)/shard_map/while/body/eval_jaxpr/sub | solution.py:110
  523.2 16.6 %fusion.56 = f32[8,32,768]{2,1,0:T(8,128)S(1)} fusion(bf16[768,8,32]{0,2,1:T(8,128)(2,1)S(1)} %bitcast.105, f32[8,768]{1,0:T(8,128)S(1)} %fusion.55, f32[8,768,768]{1,2,0:T(8,128)} %add_add_fusion.2), kind=kOutput, calls=%fused_computation.4.clone.1 | convolution fusion | flops 316152576 | bytes 20078592 | tf_op jit(solution)/shard_map/while/body/eval_jaxpr/bhqk,bkhd->bqhd/dot_general | solution.py:112
  543.7 12.1 %add_add_fusion.2 = f32[8,768,768]{1,2,0:T(8,128)} fusion(f32[8,768,768]{1,2,0:T(8,128)} %get-tuple-element.252, f32[768]{0:T(1024)S(1)} %multiply_reduce_fusion.3, bf16[768,8,32]{0,2,1:T(8,128)(2,1)S(1)} %bitcast.102, bf16[768,8,32]{0,2,1:T(8,128)(2,1)S(1)} %bitcast.103), kind=kOutput, calls=%fused_computation.3.clone.1 | convolution fusion | flops 316145664 | bytes 38538240 | tf_op jit(solution)/shard_map/while/body/eval_jaxpr/bqhd,bkhd->bhqk/dot_general | solution.py:101
  555.9 13.7 %fusion.55 = f32[8,768]{1,0:T(8,128)S(1)} fusion(f32[8,768,768]{1,2,0:T(8,128)} %add_add_fusion.2), kind=kOutput, calls=%fused_computation.61.clone.1 | output fusion | flops 9437951 | bytes 18898944 | tf_op jit(solution)/shard_map/while/body/eval_jaxpr/sub | solution.py:110
  569.8 16.6 %fusion.56 = f32[8,32,768]{2,1,0:T(8,128)S(1)} fusion(bf16[768,8,32]{0,2,1:T(8,128)(2,1)S(1)} %bitcast.105, f32[8,768]{1,0:T(8,128)S(1)} %fusion.55, f32[8,768,768]{1,2,0:T(8,128)} %add_add_fusion.2), kind=kOutput, calls=%fused_computation.4.clone.1 | convolution fusion | flops 316152576 | bytes 20078592 | tf_op jit(solution)/shard_map/while/body/eval_jaxpr/bhqk,bkhd->bqhd/dot_general | solution.py:112
  590.3 12.1 %add_add_fusion.2 = f32[8,768,768]{1,2,0:T(8,128)} fusion(f32[8,768,768]{1,2,0:T(8,128)} %get-tuple-element.252, f32[768]{0:T(1024)S(1)} %multiply_reduce_fusion.3, bf16[768,8,32]{0,2,1:T(8,128)(2,1)S(1)} %bitcast.102, bf16[768,8,32]{0,2,1:T(8,128)(2,1)S(1)} %bitcast.103), kind=kOutput, calls=%fused_computation.3.clone.1 | convolution fusion | flops 316145664 | bytes 38538240 | tf_op jit(solution)/shard_map/while/body/eval_jaxpr/bqhd,bkhd->bhqk/dot_general | solution.py:101
  602.5 13.7 %fusion.55 = f32[8,768]{1,0:T(8,128)S(1)} fusion(f32[8,768,768]{1,2,0:T(8,128)} %add_add_fusion.2), kind=kOutput, calls=%fused_computation.61.clone.1 | output fusion | flops 9437951 | bytes 18898944 | tf_op jit(solution)/shard_map/while/body/eval_jaxpr/sub | solution.py:110
  616.4 16.6 %fusion.56 = f32[8,32,768]{2,1,0:T(8,128)S(1)} fusion(bf16[768,8,32]{0,2,1:T(8,128)(2,1)S(1)} %bitcast.105, f32[8,768]{1,0:T(8,128)S(1)} %fusion.55, f32[8,768,768]{1,2,0:T(8,128)} %add_add_fusion.2), kind=kOutput, calls=%fused_computation.4.clone.1 | convolution fusion | flops 316152576 | bytes 20078592 | tf_op jit(solution)/shard_map/while/body/eval_jaxpr/bhqk,bkhd->bqhd/dot_general | solution.py:112
  636.9 23.0 %all_to_all.84 = bf16[4,768,256]{2,0,1:T(4,128)(2,1)S(1)} all-to-all(bf16[4,768,256]{2,0,1:T(4,128)(2,1)S(1)} %bitcast.110), channel_id=1, replica_groups=mesh['row'=16,'col'=8] {'col'}, dimensions={1} | all-to-all | bytes 3145728 | tf_op jit(solution)/shard_map/all_to_all | solution.py:220
  (130 shorter events, 111.0 us)
Async XLA Ops:
  7.2 264.7 %copy-start = (bf16[256,1024]{1,0:T(8,128)(2,1)S(1)}, bf16[256,1024]{1,0:T(8,128)(2,1)}, u32[]{:S(2)}) copy-start(bf16[256,1024]{1,0:T(8,128)(2,1)} %param.26) | copy-start | bytes 1572868
  7.2 2.3 copy-start.2
  7.2 3.3 copy-start.8
  7.2 3.3 copy-start.16
  7.2 3.3 copy-start.14
  7.2 52.8 %all-gather.6.cloned.1.call-start = ((), (), s32[]{:S(2)}) async-start(), calls=%async_computation.7 | async-start | bytes 1824768 | tf_op jit(solution)/shard_map/all_gather | solution.py:28
  10.6 2.9 copy-start.15
  13.4 114.8 %all-gather.4.cloned.1.call-start = ((), (), s32[]{:S(2)}) async-start(), calls=%async_computation.6 | async-start | bytes 3481600 | tf_op jit(solution)/shard_map/all_gather | solution.py:42
  65.2 15.9 %all-to-all-start.2 = ((bf16[16,2,768]{2,1,0:T(2,128)(2,1)}), bf16[16,2,768]{2,1,0:T(2,128)(2,1)S(1)}, u32[]{:S(2)}, u32[]{:S(2)}) async-start(bf16[16,2,768]{2,1,0:T(2,128)(2,1)} %reshape.229), calls=%async_computation.2 | async-start | bytes 98304 | tf_op jit(solution)/shard_map/all_to_all | solution.py:169
  81.1 7.4 %copy-start.9 = (s32[768]{0:T(1024)S(1)}, s32[768]{0:T(1024)}, u32[]{:S(2)}) copy-start(s32[768]{0:T(1024)} %param.17) | copy-start | bytes 9220
  81.1 33.8 %all-to-all-start.1 = ((bf16[32,16,1536]{2,0,1:T(8,128)(2,1)}), bf16[32,16,1536]{2,0,1:T(8,128)(2,1)}, u32[]{:S(2)}, u32[]{:S(2)}) async-start(bf16[32,16,1536]{2,0,1:T(8,128)(2,1)} %copy.86), calls=%async_computation.1 | async-start | bytes 3145728 | tf_op jit(solution)/shard_map/all_to_all | solution.py:168
  137.7 42.1 %copy-start.13 = (bf16[1024,128]{1,0:T(8,128)(2,1)S(1)}, bf16[1024,128]{1,0:T(8,128)(2,1)}, u32[]{:S(2)}) copy-start(bf16[1024,128]{1,0:T(8,128)(2,1)} %param.24) | copy-start | bytes 786436
  198.1 3.1 copy-start.4
  198.1 3.1 copy-start.10
  198.1 3.1 copy-start.12
  201.2 8.5 %copy-start.11 = (f32[256]{0:T(256)S(1)}, f32[256]{0:T(256)}, u32[]{:S(2)}) copy-start(f32[256]{0:T(256)} %param.20) | copy-start | bytes 3076
  204.2 17.7 %all-to-all-start.3 = ((bf16[8,8,48,96]{3,2,1,0:T(8,128)(2,1)}), bf16[8,8,48,96]{3,2,1,0:T(8,128)(2,1)}, u32[]{:S(2)}, u32[]{:S(2)}) async-start(bf16[8,8,48,96]{3,2,1,0:T(8,128)(2,1)} %broadcast_in_dim.6), calls=%async_computation.3 | async-start | bytes 1572864 | tf_op jit(solution)/shard_map/all_to_all | solution.py:47
  209.7 1.1 copy-start.6
  222.0 35.4 %all-to-all-start = ((bf16[32,96,257]{1,2,0:T(8,128)(2,1)}), bf16[32,96,257]{1,2,0:T(8,128)(2,1)S(1)}, u32[]{:S(2)}, u32[]{:S(2)}) async-start(bf16[32,96,257]{1,2,0:T(8,128)(2,1)} %copy.83), calls=%async_computation | async-start | bytes 4325376 | tf_op jit(solution)/shard_map/all_to_all | solution.py:58
  257.3 6.0 copy-start.5
  263.4 153.0 %all-to-all-start.4 = ((bf16[16,8,48,768]{3,2,1,0:T(8,128)(2,1)}), bf16[16,8,48,768]{3,2,1,0:T(8,128)(2,1)}, u32[]{:S(2)}, u32[]{:S(2)}) async-start(bf16[16,8,48,768]{3,2,1,0:T(8,128)(2,1)} %stack.3), calls=%async_computation.4 | async-start | bytes 18874368 | tf_op jit(solution)/shard_map/all_to_all | solution.py:13
  660.1 1.4 copy-start.3
  660.1 1.4 copy-start.7
  660.3 3.0 copy-start.1
Sparse Core Ops, SparseCore 0:
  13.6 46.4 all-gather.5
  62.5 65.7 all-gather.3
